TPU v7x, 512 devices: a whole 4x8x8 slice. The times are simulated.
512 devices in a mesh: member: 8 (over y_lo, core), slab: 64 (over y_hi, x, z).
Axes of the slice: x: 4, y: 8 (y_hi: 2, y_lo: 4; y = y_hi * 4 + y_lo), z: 8, core: 2. Of those that a mesh axis runs over, the one named last changes fastest.
Arguments:
- base_field: bfloat16 [32, 512, 2, 512], P(None, 'slab'), may hold values from -6 to 6
- forcing: bfloat16 [512, 2, 512], P('slab'), may hold values from -6 to 6
- load: float32 [32], replicated, may hold values from 0.25 to 1.75
- amplitudes: float32 [16], replicated, may hold values from 0.25 to 2
- amp_index: int32 [8], P('member'), may hold values from 0 to 15
- mode_count: int32 [8], P('member'), may hold values from 32 to 64, as said below
- point_weight: bfloat16 [32, 32], replicated, may hold values from -1 to 1
- point_bias: float32 [32], replicated, may hold values from -3 to 3
- spectral_weight: bfloat16 [64, 64, 2, 32, 32], P('slab'), may hold values from -6 to 6
Outputs:
- dependence: bfloat16 [32, 512, 2, 512], P('member', 'slab')
Inputs may be any that keep to these rules, and one draw needn't show every extreme that they name: `mode_count`: each member keeps the second-dimension modes below its count; some member keeps all 64.
All inputs are finite; a program needn't handle non-finite values.
Results may differ from a plain program's by a relative error of at most 0.015.
Values may be sent and summed in bfloat16 or wider, within the bound.
A program may use at most 64 MiB of HBM per device.

v0:
```python
import math
import jax
import jax.numpy as jnp
from jax import lax
from jax.sharding import PartitionSpec as P

TWO_PI = 2.0 * math.pi


def phases(frequency, positions, length):
    product = frequency[:, None] * positions[None, :] % length
    angles = product.astype(jnp.float32) * (TWO_PI / length)
    return (jnp.cos(angles), jnp.sin(angles))


def forward_x(pencil, cos_table, sin_table):
    row_total = pencil.shape[0]
    modes = cos_table.shape[0]
    with_cos = jnp.einsum(
        "kxf,mx->kmf", pencil, cos_table, preferred_element_type=jnp.float32
    ).reshape(row_total, modes, 2, -1)
    with_sin = jnp.einsum(
        "kxf,mx->kmf", pencil, sin_table, preferred_element_type=jnp.float32
    ).reshape(row_total, modes, 2, -1)
    real_part = with_cos[:, :, 0] + with_sin[:, :, 1]
    imag_part = with_cos[:, :, 1] - with_sin[:, :, 0]
    return jnp.stack([real_part, imag_part], axis=2).reshape(row_total, modes, -1)


def inverse_x(spectra, cos_table, sin_table):
    row_total = spectra.shape[0]
    points = cos_table.shape[1]
    with_cos = jnp.einsum(
        "kmf,mx->kxf", spectra, cos_table, preferred_element_type=jnp.float32
    ).reshape(row_total, points, 2, -1)
    with_sin = jnp.einsum(
        "kmf,mx->kxf", spectra, sin_table, preferred_element_type=jnp.float32
    ).reshape(row_total, points, 2, -1)
    real_part = with_cos[:, :, 0] - with_sin[:, :, 1]
    imag_part = with_cos[:, :, 1] + with_sin[:, :, 0]
    return jnp.stack([real_part, imag_part], axis=2).reshape(row_total, points, -1)


def mixing(weights, values):
    return jnp.einsum("kmoi,kmiz->kmoz", weights, values, preferred_element_type=jnp.float32)


def local(
    base_field,
    forcing,
    load,
    amplitudes,
    amp_index,
    mode_count,
    point_weight,
    point_bias,
    spectral_weight,
):
    channels, slab_rows, plane_count, length_y = base_field.shape
    slab_count = lax.axis_size("slab")
    local_modes = spectral_weight.shape[0]
    modes_y = local_modes * slab_count
    modes_x = spectral_weight.shape[1]
    length_x = slab_rows * slab_count
    packed_width = 2 * channels * plane_count
    slab_index = lax.axis_index("slab")
    level_ids = jnp.arange(amplitudes.shape[0], dtype=jnp.int32)
    amplitude = jnp.sum(jnp.where(level_ids == amp_index[0], amplitudes, 0.0))
    driven = base_field.astype(jnp.float32) + amplitude * load[:, None, None, None] * forcing[
        None
    ].astype(jnp.float32)
    field_now = (2.0 * jnp.tanh(0.5 * driven)).astype(jnp.bfloat16)
    y_cos, y_sin = phases(
        jnp.arange(modes_y, dtype=jnp.int32), jnp.arange(length_y, dtype=jnp.int32), length_y
    )
    y_real = jnp.einsum(
        "cxzy,ky->kxcz", field_now, y_cos.astype(jnp.bfloat16), preferred_element_type=jnp.float32
    )
    y_imag = -jnp.einsum(
        "cxzy,ky->kxcz", field_now, y_sin.astype(jnp.bfloat16), preferred_element_type=jnp.float32
    )
    packed = (
        jnp.stack([y_real, y_imag], axis=2)
        .astype(jnp.bfloat16)
        .reshape(modes_y, slab_rows, packed_width)
    )
    frequency_x = jnp.concatenate(
        [
            jnp.arange(modes_x // 2, dtype=jnp.int32),
            jnp.arange(length_x - modes_x // 2, length_x, dtype=jnp.int32),
        ]
    )
    local_points = slab_index * slab_rows + jnp.arange(slab_rows, dtype=jnp.int32)
    part_cos, part_sin = phases(frequency_x, local_points, length_x)
    part_cos = part_cos.astype(jnp.bfloat16)
    part_sin = part_sin.astype(jnp.bfloat16)
    full_cos, full_sin = phases(frequency_x, jnp.arange(length_x, dtype=jnp.int32), length_x)
    full_cos = full_cos.astype(jnp.bfloat16)
    full_sin = full_sin.astype(jnp.bfloat16)
    spectrum = lax.psum_scatter(
        forward_x(packed, part_cos, part_sin), "slab", scatter_dimension=0, tiled=True
    )
    spectrum = spectrum.astype(jnp.bfloat16).reshape(local_modes, modes_x, 2, channels, plane_count)
    weight_real = spectral_weight[:, :, 0]
    weight_imag = spectral_weight[:, :, 1]
    spec_real = spectrum[:, :, 0]
    spec_imag = spectrum[:, :, 1]
    mix_real = mixing(weight_real, spec_real) - mixing(weight_imag, spec_imag)
    mix_imag = mixing(weight_real, spec_imag) + mixing(weight_imag, spec_real)
    global_modes = slab_index * local_modes + jnp.arange(local_modes, dtype=jnp.int32)
    keep = (global_modes < mode_count[0]).astype(jnp.float32)[:, None, None, None, None]
    mixed = (
        (jnp.stack([mix_real, mix_imag], axis=2) * keep)
        .astype(jnp.bfloat16)
        .reshape(local_modes, modes_x, packed_width)
    )
    returned = inverse_x(
        lax.all_gather(mixed, "slab", axis=0, tiled=True), part_cos, part_sin
    ).astype(jnp.bfloat16)
    returned = returned.reshape(modes_y, slab_rows, 2, channels, plane_count)
    weights_y = jnp.where(jnp.arange(modes_y) == 0, 1.0, 2.0).astype(jnp.float32) / (
        length_x * length_y
    )
    back_cos = (weights_y[:, None] * y_cos).astype(jnp.bfloat16)
    back_sin = (weights_y[:, None] * y_sin).astype(jnp.bfloat16)
    spectral = jnp.einsum(
        "kxcz,ky->cxzy", returned[:, :, 0], back_cos, preferred_element_type=jnp.float32
    )
    spectral = spectral - jnp.einsum(
        "kxcz,ky->cxzy", returned[:, :, 1], back_sin, preferred_element_type=jnp.float32
    )
    pointwise = (
        jnp.einsum("oc,cxzy->oxzy", point_weight, field_now, preferred_element_type=jnp.float32)
        + point_bias[:, None, None, None]
    )
    layer = jax.nn.gelu(pointwise + spectral, approximate=True).astype(jnp.bfloat16)
    layer = lax.optimization_barrier(layer).astype(jnp.float32)
    total = lax.psum_scatter(
        layer.astype(jnp.bfloat16), "member", scatter_dimension=0, tiled=True
    ).astype(jnp.float32)
    return (total / lax.axis_size("member")).astype(jnp.bfloat16)


def solution(mesh):
    in_specs = (
        P(None, "slab", None, None),
        P("slab", None, None),
        P(),
        P(),
        P("member"),
        P("member"),
        P(),
        P(),
        P("slab", None, None, None, None),
    )
    out_specs = P("member", "slab", None, None)
    return jax.shard_map(local, mesh=mesh, in_specs=in_specs, out_specs=out_specs, check_vma=False)
```

profile of v0, /device:TPU:2, one launch (start us, length us, event | category | flops | bytes accessed | tf_op | source)
XLA Modules:
  0.0 677.5 jit_solution(10603344090468271848)
XLA Ops:
  7.9 1.3 fusion.62
  9.3 1.3 broadcast_multiply_fusion
  10.5 1.4 multiply_convert_fusion
  12.0 0.8 fusion.4
  12.8 0.8 fusion.5
  14.1 1.9 convolution_bitcast_fusion.1
  16.6 5.8 reshape.104
  22.4 3.7 reshape.105
  26.1 11.8 %slice_add_fusion = (f32[64,64,1,64]{3,2,1,0:T(1,128)S(1)}, f32[64,64,1,64]{3,2,1,0:T(1,128)S(1)}) fusion(f32[64,64,2,64]{3,2,1,0:T(2,128)} %reshape.105, f32[64,64,2,64]{3,2,1,0:T(2,128)} %reshape.104), kind=kLoop, calls=%fused_computation.2 | loop fusion | flops 524288 | bytes 6291456 | tf_op jit(solution)/shard_map/add | solution.py:25
  37.9 6.8 %pad_maximum_fusion = f32[64,64,2,64]{3,2,1,0:T(2,128)} fusion(f32[64,64,1,64]{3,2,1,0:T(1,128)S(1)} %get-tuple-element.6, f32[64,64,1,64]{3,2,1,0:T(1,128)S(1)} %get-tuple-element.5), kind=kLoop, calls=%fused_computation | loop fusion | flops 524288 | bytes 4194304 | tf_op jit(solution)/shard_map/stack | solution.py:27
  44.7 7.2 %copy.55 = f32[64,64,2,64]{1,3,2,0:T(8,128)} copy(f32[64,64,2,64]{3,2,1,0:T(2,128)} %pad_maximum_fusion) | data formatting | bytes 4194304 | tf_op jit(solution)/shard_map/stack | solution.py:27
  52.2 0.7 copy-done.3
  53.0 0.8 copy.84
  53.8 0.8 copy.82
  55.3 422.5 %reduce-scatter.3.cloned.1.call-done = f32[1,64,128]{1,2,0:T(8,128)} async-done(((f32[64,64,128]{1,2,0:T(8,128)}), f32[1,64,128]{1,2,0:T(8,128)}) %reduce-scatter.3.cloned.1.call-update) | async-done | bytes 32784 | tf_op jit(solution)/shard_map/reduce_scatter | solution.py:100
  477.8 0.8 convert_element_type.91
  481.6 1.3 fusion.2
  482.9 148.2 %all-gather.2.cloned.1.call-done = bf16[64,64,128]{2,1,0:T(8,128)(2,1)} async-done(((bf16[1,64,128]{2,1,0:T(8,128)(2,1)}), bf16[64,64,128]{2,1,0:T(8,128)(2,1)}) %all-gather.2.cloned.1.call-update) | async-done | bytes 1048592 | tf_op jit(solution)/shard_map/all_gather | solution.py:118
  631.1 1.7 convolution_bitcast_fusion.3
  633.8 0.8 fusion.27
  634.6 1.0 fusion.13
  635.6 1.1 copy.72
  636.7 32.7 %reduce-scatter.5.cloned.1.call-done = bf16[4,8,2,512]{3,1,2,0:T(8,128)(2,1)} async-done(((bf16[32,8,2,512]{3,1,2,0:T(8,128)(2,1)}), bf16[4,8,2,512]{3,1,2,0:T(8,128)(2,1)}) %reduce-scatter.5.cloned.1.call-update) | async-done | bytes 65552 | tf_op jit(solution)/shard_map/reduce_scatter | solution.py:138
  669.5 0.9 multiply_convert_fusion.1
  (48 shorter events, 6.9 us)
Async XLA Ops:
  6.5 475.1 %copy-start = (bf16[32,32]{1,0:T(8,128)(2,1)S(1)}, bf16[32,32]{1,0:T(8,128)(2,1)}, u32[]{:S(2)}) copy-start(bf16[32,32]{1,0:T(8,128)(2,1)} %param.15) | copy-start | bytes 6148
  6.5 471.2 %reduce-scatter.3.cloned.1.call-start = ((), (), s32[]{:S(2)}) async-start(), calls=%async_computation.2 | async-start | bytes 4259840 | tf_op jit(solution)/shard_map/reduce_scatter | solution.py:100
  51.9 1.0 copy-start.3
  52.0 579.1 %all-gather.2.cloned.1.call-start = ((), (), s32[]{:S(2)}) async-start(), calls=%async_computation.3 | async-start | bytes 1064960 | tf_op jit(solution)/shard_map/all_gather | solution.py:118
  53.8 427.8 %copy-start.4 = (f32[32]{0:T(128)S(1)}, f32[32]{0:T(128)}, u32[]{:S(2)}) copy-start(f32[32]{0:T(128)} %param.16) | copy-start | bytes 388
  481.5 187.9 %reduce-scatter.5.cloned.1.call-start = ((), (), s32[]{:S(2)}) async-start(), calls=%async_computation.4 | async-start | bytes 589824 | tf_op jit(solution)/shard_map/reduce_scatter | solution.py:138
  631.1 1.9 copy-start.1
  633.4 1.2 copy-start.2
Sparse Core Ops, SparseCore 0:
  52.1 425.6 reduce-scatter.2
  482.9 148.1 all-gather.1
  636.9 32.5 reduce-scatter.4
where the time goes:
time: 678 us
  waiting for transfers between devices  603 us (89%)
  other arithmetic  25.4 us (4%)
  local copies, waits for them, and re-layouts  23.1 us (3%)
  between operations  14.6 us (2%)
  matrix products  10.6 us (2%)
    reduce_scatter x1, waiting for transfers between devices, local(): lax.psum_scatter(forward_x(packed, part_cos, part_sin), 'slab', scatter_d...  423 us
    all_gather x1, waiting for transfers between devices, local(): lax.all_gather(mixed, 'slab', axis=0, tiled=True)  148 us
    reduce_scatter x1, waiting for transfers between devices, local(): lax.psum_scatter(layer.astype(jnp.bfloat16), 'member', scatter_dimension=...  32.7 us
  transfers between devices with their start and end apart: 3, of which 3 were waited for; matrix products, arithmetic and copies ran while one was open for 0% of the time, Pallas kernels for 0%

commit v1 on v0

--- a/solution.py
+++ b/solution.py
@@ -115,7 +115,11 @@
         .reshape(local_modes, modes_x, packed_width)
     )
     returned = inverse_x(
-        lax.all_gather(mixed, "slab", axis=0, tiled=True), part_cos, part_sin
+        jnp.concatenate(
+            lax.all_to_all(jnp.stack([mixed] * lax.axis_size("slab")), "slab", 0, 0), axis=0
+        ),
+        part_cos,
+        part_sin,
     ).astype(jnp.bfloat16)
     returned = returned.reshape(modes_y, slab_rows, 2, channels, plane_count)
     weights_y = jnp.where(jnp.arange(modes_y) == 0, 1.0, 2.0).astype(jnp.float32) / (

time: 678 us -> 590 us (0.87)
  waiting for transfers between devices: 603 us -> 479 us
  starting transfers between devices: 0.31 us -> 36.9 us
    all_gather x1 -> x0, waiting for transfers between devices: 148 us -> none  [local(): lax.all_gather(mixed, 'slab', axis=0, tiled=True)]
    all_to_all x0 -> x1, starting transfers between devices: none -> 36.9 us  [local(): lax.all_to_all(jnp.stack([mixed] * lax.axis_size('slab')), 'slab', 0, 0)]
    all_to_all x0 -> x1, waiting for transfers between devices: none -> 19 us  [local(): lax.all_to_all(jnp.stack([mixed] * lax.axis_size('slab')), 'slab', 0, 0)]
where the time goes in v1:
time: 590 us; the launch traced here: 589 us
  waiting for transfers between devices  479 us (81%)
  starting transfers between devices  36.9 us (6%)
  other arithmetic  25.4 us (4%)
  local copies, waits for them, and re-layouts  24.1 us (4%)
  between operations  14.9 us (3%)
  matrix products  9.22 us (2%)
    reduce_scatter x1, waiting for transfers between devices, local(): lax.psum_scatter(forward_x(packed, part_cos, part_sin), 'slab', scatter_d...  425 us
    all_to_all x1, starting transfers between devices, local(): lax.all_to_all(jnp.stack([mixed] * lax.axis_size('slab')), 'slab', 0, 0)  36.9 us
    reduce_scatter x1, waiting for transfers between devices, local(): lax.psum_scatter(layer.astype(jnp.bfloat16), 'member', scatter_dimension=...  34.9 us
    all_to_all x1, waiting for transfers between devices, local(): lax.all_to_all(jnp.stack([mixed] * lax.axis_size('slab')), 'slab', 0, 0)  19 us
  transfers between devices with their start and end apart: 3, of which 3 were waited for; matrix products, arithmetic and copies ran while one was open for 0% of the time, Pallas kernels for 0%

profile of v1, /device:TPU:2, one launch (start us, length us, event | category | flops | bytes accessed | tf_op | source)
XLA Modules:
  0.0 589.1 jit_solution(3971294159763307790)
XLA Ops:
  7.9 1.3 fusion.64
  9.2 1.3 broadcast_multiply_fusion
  10.5 1.4 multiply_convert_fusion
  12.7 0.8 fusion.5
  14.1 1.9 convolution_bitcast_fusion.1
  16.6 5.8 reshape.102
  22.4 3.7 reshape.103
  26.1 11.8 %slice_add_fusion = (f32[64,64,1,64]{3,2,1,0:T(1,128)S(1)}, f32[64,64,1,64]{3,2,1,0:T(1,128)S(1)}) fusion(f32[64,64,2,64]{3,2,1,0:T(2,128)} %reshape.103, f32[64,64,2,64]{3,2,1,0:T(2,128)} %reshape.102), kind=kLoop, calls=%fused_computation.2 | loop fusion | flops 524288 | bytes 6291456 | tf_op jit(solution)/shard_map/add | solution.py:25
  37.9 6.8 %pad_maximum_fusion = f32[64,64,2,64]{3,2,1,0:T(2,128)} fusion(f32[64,64,1,64]{3,2,1,0:T(1,128)S(1)} %get-tuple-element.6, f32[64,64,1,64]{3,2,1,0:T(1,128)S(1)} %get-tuple-element.5), kind=kLoop, calls=%fused_computation | loop fusion | flops 524288 | bytes 4194304 | tf_op jit(solution)/shard_map/stack | solution.py:27
  44.7 7.2 %copy.55 = f32[64,64,2,64]{1,3,2,0:T(8,128)} copy(f32[64,64,2,64]{3,2,1,0:T(2,128)} %pad_maximum_fusion) | data formatting | bytes 4194304 | tf_op jit(solution)/shard_map/stack | solution.py:27
  52.0 1.0 copy-done.2
  53.0 0.8 copy.84
  53.8 0.8 copy.82
  55.3 424.6 %reduce-scatter.3.cloned.1.call-done = f32[1,64,128]{1,2,0:T(8,128)} async-done(((f32[64,64,128]{1,2,0:T(8,128)}), f32[1,64,128]{1,2,0:T(8,128)}) %reduce-scatter.3.cloned.1.call-update) | async-done | bytes 32784 | tf_op jit(solution)/shard_map/reduce_scatter | solution.py:100
  479.8 0.8 convert_element_type.89
  482.9 1.3 stack.42
  484.2 36.9 %all-to-all-start = ((bf16[64,1,64,128]{3,2,1,0:T(8,128)(2,1)}), bf16[64,1,64,128]{3,2,1,0:T(8,128)(2,1)S(1)}, u32[]{:S(2)}, u32[]{:S(2)}) async-start(bf16[64,1,64,128]{3,2,1,0:T(8,128)(2,1)} %stack.42), calls=%async_computation.1 | async-start | bytes 2097152 | tf_op jit(solution)/shard_map/all_to_all | solution.py:119
  521.2 1.2 fusion.2
  522.4 19.0 %all-to-all-done = bf16[64,1,64,128]{3,2,1,0:T(8,128)(2,1)S(1)} async-done(((bf16[64,1,64,128]{3,2,1,0:T(8,128)(2,1)}), bf16[64,1,64,128]{3,2,1,0:T(8,128)(2,1)S(1)}, u32[]{:S(2)}, u32[]{:S(2)}) %all-to-all-start) | async-done | bytes 1048608 | tf_op jit(solution)/shard_map/all_to_all | solution.py:119
  542.9 0.8 fusion.29
  543.7 1.0 fusion.13
  544.7 1.1 copy.72
  545.8 34.9 %reduce-scatter.5.cloned.1.call-done = bf16[4,8,2,512]{3,1,2,0:T(8,128)(2,1)} async-done(((bf16[32,8,2,512]{3,1,2,0:T(8,128)(2,1)}), bf16[4,8,2,512]{3,1,2,0:T(8,128)(2,1)}) %reduce-scatter.5.cloned.1.call-update) | async-done | bytes 65552 | tf_op jit(solution)/shard_map/reduce_scatter | solution.py:142
  580.7 0.9 multiply_convert_fusion.1
  (46 shorter events, 7.1 us)
Async XLA Ops:
  6.5 514.6 %copy-start = (bf16[32,32]{1,0:T(8,128)(2,1)S(1)}, bf16[32,32]{1,0:T(8,128)(2,1)}, u32[]{:S(2)}) copy-start(bf16[32,32]{1,0:T(8,128)(2,1)} %param.15) | copy-start | bytes 6148
  6.5 473.3 %reduce-scatter.3.cloned.1.call-start = ((), (), s32[]{:S(2)}) async-start(), calls=%async_computation.3 | async-start | bytes 4259840 | tf_op jit(solution)/shard_map/reduce_scatter | solution.py:100
  52.0 1.0 copy-start.2
  482.4 38.8 %copy-start.3 = (f32[32]{0:T(128)S(1)}, f32[32]{0:T(128)}, u32[]{:S(2)}) copy-start(f32[32]{0:T(128)} %param.16) | copy-start | bytes 388
  484.2 57.2 %all-to-all-start = ((bf16[64,1,64,128]{3,2,1,0:T(8,128)(2,1)}), bf16[64,1,64,128]{3,2,1,0:T(8,128)(2,1)S(1)}, u32[]{:S(2)}, u32[]{:S(2)}) async-start(bf16[64,1,64,128]{3,2,1,0:T(8,128)(2,1)} %stack.42), calls=%async_computation.1 | async-start | bytes 2097152 | tf_op jit(solution)/shard_map/all_to_all | solution.py:119
  521.1 59.6 %reduce-scatter.5.cloned.1.call-start = ((), (), s32[]{:S(2)}) async-start(), calls=%async_computation.4 | async-start | bytes 589824 | tf_op jit(solution)/shard_map/reduce_scatter | solution.py:142
  542.4 1.2 copy-start.1
Sparse Core Ops, SparseCore 0:
  52.1 427.6 reduce-scatter.2
  545.9 34.7 reduce-scatter.4
